TPU v7x, 128 devices: a whole 4x4x4 slice. The times are simulated.
128 devices in a mesh: expert: 16 (over y, z_lo, core), shard: 8 (over z_hi, x).
Axes of the slice: x: 4, y: 4, z: 4 (z_hi: 2, z_lo: 2; z = z_hi * 2 + z_lo), core: 2. Of those that a mesh axis runs over, the one named last changes fastest.
Arguments:
- tokens: bfloat16 [16384, 2048], P(('expert', 'shard')), may hold values from -6 to 6
- expert_ids: int32 [16384, 4], P(('expert', 'shard')), may hold values from 0 to 15, all different within a row; in each aligned block of 128 rows (0 to 127, 128 to 255, ...) at most 48 rows name the same one
- route_weights: float32 [16384, 4], P(('expert', 'shard')), may hold values from 0.1 to 1
- partner: int32 [16], replicated, may hold values from 0 to 15, as said below
- w_in: bfloat16 [16, 2, 2048, 768], P('expert', None, 'shard'), may hold values from -0.125 to 0.125
- w_down: bfloat16 [16, 768, 2048], P('expert', None, 'shard'), may hold values from -0.21875 to 0.21875
- m_in: float32 [16, 2, 2048, 768], P('expert', None, 'shard'), may hold values from -6 to 6
- v_in: float32 [16, 2, 2048, 768], P('expert', None, 'shard'), may hold values from 0.01 to 1
- m_down: float32 [16, 768, 2048], P('expert', None, 'shard'), may hold values from -6 to 6
- v_down: float32 [16, 768, 2048], P('expert', None, 'shard'), may hold values from 0.01 to 1
- cotangent: bfloat16 [16384, 2048], P(('expert', 'shard')), may hold values from -6 to 6
Outputs:
- mixed: bfloat16 [16384, 2048], P(('expert', 'shard'))
- token_grad: bfloat16 [16384, 2048], P(('expert', 'shard'))
- new_w_in: bfloat16 [16, 2, 2048, 768], P('expert', None, 'shard')
- new_w_down: bfloat16 [16, 768, 2048], P('expert', None, 'shard')
- new_m_in: float32 [16, 2, 2048, 768], P('expert', None, 'shard')
- new_v_in: float32 [16, 2, 2048, 768], P('expert', None, 'shard')
- new_m_down: float32 [16, 768, 2048], P('expert', None, 'shard')
- new_v_down: float32 [16, 768, 2048], P('expert', None, 'shard')
Inputs may be any that keep to these rules, and one draw needn't show every extreme that they name: `expert_ids`: within the rows of one device no expert is named more than 48 times, a bound that some block reaches. partner[g] is g or (g + 8) mod 16, and partner[partner[g]] = g; partner[0] is 8.
All inputs are finite; a program needn't handle non-finite values.
Results may differ from a plain program's by a relative error of at most 0.024.
Values may be sent and summed in bfloat16 or wider, within the bound.
A program may use at most 128 MiB of HBM per device.

v0:
```python
import jax
import jax.numpy as jnp
from jax import lax
from jax.sharding import PartitionSpec as P

beta_first = 0.9
beta_second = 0.999
learn_rate = 0.01
adam_eps = 1e-08
bias_first = 0.9999734386011124
bias_second = 0.09520785288629038


def shifted(block, axis, distance):
    devices = range(lax.axis_size(axis))
    route = [((i - distance) % len(devices), i) for i in devices]
    return lax.ppermute(block, axis, route)


def silu_parts(gate_pre):
    sigmoid_value = jax.nn.sigmoid(gate_pre)
    silu_value = gate_pre * sigmoid_value
    slope = sigmoid_value * (1.0 + gate_pre * (1.0 - sigmoid_value))
    return (silu_value, slope)


def adam_update(weight, first, second, grad):
    first_new = beta_first * first + (1.0 - beta_first) * grad
    second_new = beta_second * second + (1.0 - beta_second) * grad * grad
    update = learn_rate * (first_new / bias_first) / (jnp.sqrt(second_new / bias_second) + adam_eps)
    return ((weight.astype(jnp.float32) - update).astype(jnp.bfloat16), first_new, second_new)


def route_table(expert_ids, dest_rows, groups, capacity):
    entry_count = expert_ids.shape[0] * expert_ids.shape[1]
    flat_ids = expert_ids.reshape(entry_count)
    onehot = (flat_ids[:, None] == jnp.arange(groups, dtype=jnp.int32)[None, :]).astype(jnp.int32)
    before = jnp.cumsum(onehot, axis=0) - onehot
    slot_index = jnp.sum(before * onehot, axis=1)
    position = dest_rows.reshape(entry_count) * capacity + slot_index
    entry_index = jnp.arange(entry_count, dtype=jnp.int32)
    filler = jnp.full((groups * capacity,), -1, jnp.int32).at[position].set(entry_index)
    return (position, filler)


def fill_rows(source_rows, filler, groups, capacity):
    picked = jnp.take(source_rows, jnp.maximum(filler, 0), axis=0)
    kept = jnp.where((filler >= 0)[:, None], picked, jnp.zeros_like(picked))
    return kept.reshape(groups, capacity, source_rows.shape[1])


def contract_rows(left, right):
    return lax.dot_general(
        left, right, (((0,), (0,)), ((), ())), preferred_element_type=jnp.float32
    )


def contract_cols(left, right):
    return lax.dot_general(
        left, right, (((1,), (1,)), ((), ())), preferred_element_type=jnp.float32
    )


def body(
    tokens, expert_ids, route_weights, partner, w_in, w_down, m_in, v_in, m_down, v_down, cotangent
):
    groups = lax.axis_size("expert")
    halfway = groups // 2
    tok_rows = tokens.shape[0]
    width = tokens.shape[1]
    top_count = expert_ids.shape[1]
    capacity = 3 * tok_rows * top_count // (2 * groups)
    row_index = lax.axis_index("expert")
    expert_range = jnp.arange(groups, dtype=jnp.int32)
    own_partner = jnp.sum(jnp.where(expert_range == row_index, partner, 0))
    take_other = own_partner != row_index
    moved_weights = shifted((w_in, w_down), "expert", halfway)
    w_in, w_down = (
        jnp.where(take_other, moved, owned) for moved, owned in zip(moved_weights, (w_in, w_down))
    )
    moved_states = tuple(
        (
            shifted(state.astype(jnp.bfloat16), "expert", halfway).astype(state.dtype)
            for state in (m_in, v_in, m_down, v_down)
        )
    )
    m_in, v_in, m_down, v_down = (
        jnp.where(take_other, moved, owned)
        for moved, owned in zip(moved_states, (m_in, v_in, m_down, v_down))
    )
    in_full, down_full = (
        lax.all_gather(w_in, "shard", axis=2, tiled=True),
        lax.all_gather(w_down, "shard", axis=2, tiled=True),
    )
    gate_weight = in_full[0, 0]
    up_weight = in_full[0, 1]
    down_weight = down_full[0]
    hidden_width = gate_weight.shape[1]
    position, filler = route_table(expert_ids, partner[expert_ids], groups, capacity)
    token_fill = jnp.where(filler >= 0, filler // top_count, -1)
    send_rows = fill_rows(tokens, token_fill, groups, capacity)
    arrived = lax.all_to_all(send_rows, "expert", split_axis=0, concat_axis=0, tiled=True)
    rows_x = arrived.reshape(groups * capacity, width)
    own_moments = (m_in, v_in, m_down, v_down)
    gate_pre = jnp.dot(rows_x, gate_weight, preferred_element_type=jnp.float32)
    up_pre = jnp.dot(rows_x, up_weight, preferred_element_type=jnp.float32)
    silu_value, slope = silu_parts(gate_pre)
    hidden = (silu_value * up_pre).astype(jnp.bfloat16)
    expert_out = jnp.dot(hidden, down_weight, preferred_element_type=jnp.float32).astype(
        jnp.bfloat16
    )
    returned = lax.all_to_all(
        expert_out.reshape(groups, capacity, width),
        "expert",
        split_axis=0,
        concat_axis=0,
        tiled=True,
    )
    per_entry = jnp.take(returned.reshape(groups * capacity, width), position, axis=0).reshape(
        tok_rows, top_count, width
    )
    mixed = jnp.sum(route_weights[:, :, None] * per_entry.astype(jnp.float32), axis=1).astype(
        jnp.bfloat16
    )
    scaled = (route_weights[:, :, None] * cotangent[:, None, :].astype(jnp.float32)).astype(
        jnp.bfloat16
    )
    send_grads = fill_rows(scaled.reshape(tok_rows * top_count, width), filler, groups, capacity)
    dout_rows = lax.all_to_all(
        send_grads, "expert", split_axis=0, concat_axis=0, tiled=True
    ).reshape(groups * capacity, width)
    grad_hidden = contract_cols(dout_rows, down_weight)
    grad_gate = (grad_hidden * up_pre * slope).astype(jnp.bfloat16)
    grad_up = (grad_hidden * silu_value).astype(jnp.bfloat16)
    entry_grads = (
        contract_cols(grad_gate, gate_weight) + contract_cols(grad_up, up_weight)
    ).astype(jnp.bfloat16)
    back_rows = lax.all_to_all(
        entry_grads.reshape(groups, capacity, width),
        "expert",
        split_axis=0,
        concat_axis=0,
        tiled=True,
    )
    per_back = jnp.take(back_rows.reshape(groups * capacity, width), position, axis=0).reshape(
        tok_rows, top_count, width
    )
    token_grad = jnp.sum(per_back.astype(jnp.float32), axis=1).astype(jnp.bfloat16)
    grad_both = jnp.concatenate([grad_gate, grad_up], axis=1)
    share_rows = width // lax.axis_size("shard")
    shares = lax.psum_scatter(
        jnp.concatenate(
            [contract_rows(rows_x, grad_both), contract_rows(dout_rows, hidden)], axis=1
        ).astype(jnp.bfloat16),
        "shard",
        scatter_dimension=0,
        tiled=True,
    ).astype(jnp.float32)
    grad_in = jnp.transpose(
        shares[:, : 2 * hidden_width].reshape(share_rows, 2, hidden_width), (1, 0, 2)
    )[None]
    grad_down = jnp.transpose(shares[:, 2 * hidden_width :])[None]
    new_in, first_in, second_in = adam_update(w_in, own_moments[0], own_moments[1], grad_in)
    new_down, first_down, second_down = adam_update(
        w_down, own_moments[2], own_moments[3], grad_down
    )
    return (mixed, token_grad, new_in, new_down, first_in, second_in, first_down, second_down)


def solution(mesh):
    placed = (
        P(("expert", "shard"), None),
        P(("expert", "shard"), None),
        P(("expert", "shard"), None),
        P(),
        P("expert", None, "shard", None),
        P("expert", None, "shard"),
        P("expert", None, "shard", None),
        P("expert", None, "shard", None),
        P("expert", None, "shard"),
        P("expert", None, "shard"),
        P(("expert", "shard"), None),
    )
    return jax.shard_map(
        body,
        mesh=mesh,
        in_specs=placed,
        out_specs=(
            P(("expert", "shard"), None),
            P(("expert", "shard"), None),
            P("expert", None, "shard", None),
            P("expert", None, "shard"),
            P("expert", None, "shard", None),
            P("expert", None, "shard", None),
            P("expert", None, "shard"),
            P("expert", None, "shard"),
        ),
        check_vma=False,
    )
```

profile of v0, /device:TPU:1, one launch (start us, length us, event | category | flops | bytes accessed | tf_op | source)
XLA Modules:
  0.0 460.8 jit_solution(10623074164776586844)
XLA Ops:
  7.2 3.8 collective-permute-start.1
  11.1 1.3 fusion.23
  13.0 6.8 %collective-permute-done.1 = bf16[1,768,256]{2,1,0:T(8,128)(2,1)S(1)} collective-permute-done((bf16[1,768,256]{2,1,0:T(8,128)(2,1)}, bf16[1,768,256]{2,1,0:T(8,128)(2,1)S(1)}, u32[]{:S(2)}, u32[]{:S(2)}) %collective-permute-start.1) | collective-permute-done | bytes 393248 | tf_op jit(solution)/shard_map/ppermute | solution.py:17
  19.8 0.8 broadcast_select_fusion.2
  20.7 3.0 collective-permute-start
  23.7 16.4 %collective-permute-done = bf16[1,2,256,768]{3,2,1,0:T(8,128)(2,1)S(1)} collective-permute-done((bf16[1,2,256,768]{3,2,1,0:T(8,128)(2,1)}, bf16[1,2,256,768]{3,2,1,0:T(8,128)(2,1)S(1)}, u32[]{:S(2)}, u32[]{:S(2)}) %collective-permute-start) | collective-permute-done | bytes 786464 | tf_op jit(solution)/shard_map/ppermute | solution.py:17
  40.1 1.0 broadcast_select_fusion.1
  41.1 0.1 copy.23
  41.3 0.1 eq.35
  41.5 3.1 mul.160
  44.5 5.3 %mul.161 = f32[512,2048]{1,0:T(8,128)} reshape(f32[128,4,2048]{2,1,0:T(4,128)} %mul.160) | data formatting | bytes 8388608 | tf_op jit(solution)/shard_map/mul | solution.py:125
  49.9 0.1 copy.21
  50.1 0.7 fusion.27
  50.8 10.2 %select_multiply_fusion = s32[128,4]{0,1:T(4,128)S(1)} fusion(s32[128,4]{0,1:T(4,128)S(1)} %copy-done.14, s32[]{:T(128)} %bitcast, s32[]{:T(128)} %bitcast.1, s32[]{:T(128)} %bitcast.2, s32[]{:T(128)} %bitcast.3, s32[]{:T(128)} %bitcast.4, s32[]{:T(128)} %bitcast.5, s32[]{:T(128)} %bitcast.6, s32[]{:T(128)} %bitcast.7, s32[]{:T(128)} %bitcast.8, s32[]{:T(128)} %bitcast.9, ...), kind=kLoop, calls=%fused_computation.69 | loop fusion | flops 17408 | bytes 4160 | tf_op jit(solution)/shard_map/mul | solution.py:40
  61.0 0.1 copy.22
  61.1 0.1 mul.152
  61.2 1.2 reduce-window.6
  62.4 0.2 slice_reduce_fusion
  62.8 2.4 scatter_custom_fusion
  65.5 2.5 multiply_convert_fusion
  67.9 4.3 gather_fusion.1
  72.2 3.4 select_select_fusion
  75.5 9.0 %all-to-all-start.2 = ((bf16[16,48,2048]{2,1,0:T(8,128)(2,1)}), bf16[16,48,2048]{2,1,0:T(8,128)(2,1)}, u32[]{:S(2)}, u32[]{:S(2)}) async-start(bf16[16,48,2048]{2,1,0:T(8,128)(2,1)} %select_select_fusion), calls=%async_computation.2 | async-start | bytes 6291456 | tf_op jit(solution)/shard_map/all_to_all | solution.py:129
  84.7 4.3 gather_fusion
  89.0 3.4 select_select_fusion.1
  92.4 32.1 %all-to-all-done.2 = bf16[16,48,2048]{2,1,0:T(8,128)(2,1)} async-done(((bf16[16,48,2048]{2,1,0:T(8,128)(2,1)}), bf16[16,48,2048]{2,1,0:T(8,128)(2,1)}, u32[]{:S(2)}, u32[]{:S(2)}) %all-to-all-start.2) | async-done | bytes 3145760 | tf_op jit(solution)/shard_map/all_to_all | solution.py:129
  124.6 8.0 %all-to-all-start = ((bf16[16,48,2048]{2,1,0:T(8,128)(2,1)}), bf16[16,48,2048]{2,1,0:T(8,128)(2,1)S(1)}, u32[]{:S(2)}, u32[]{:S(2)}) async-start(bf16[16,48,2048]{2,1,0:T(8,128)(2,1)} %select_select_fusion.1), calls=%async_computation | async-start | bytes 6291456 | tf_op jit(solution)/shard_map/all_to_all | solution.py:102
  132.6 0.3 reduce-scatter.2.cloned.1.call-start
  133.0 7.0 %fusion = f32[768,768]{0,1:T(8,128)} fusion(bf16[768,2048]{1,0:T(8,128)(2,1)} %bitcast.27, bf16[1,768,2048]{2,1,0:T(8,128)(2,1)} %all-gather.5.cloned.1.call-done), kind=kOutput, calls=%fused_computation.14 | convolution fusion | flops 2415919104 | bytes 8650752 | tf_op jit(solution)/shard_map/dot_general | solution.py:59
  140.0 32.7 %all-to-all-done = bf16[16,48,2048]{2,1,0:T(8,128)(2,1)S(1)} async-done(((bf16[16,48,2048]{2,1,0:T(8,128)(2,1)}), bf16[16,48,2048]{2,1,0:T(8,128)(2,1)S(1)}, u32[]{:S(2)}, u32[]{:S(2)}) %all-to-all-start) | async-done | bytes 3145760 | tf_op jit(solution)/shard_map/all_to_all | solution.py:102
  172.7 46.9 %all-gather.3.cloned.1.call-done = bf16[1,2,2048,768]{3,2,1,0:T(8,128)(2,1)} async-done(((bf16[1,2,256,768]{3,2,1,0:T(8,128)(2,1)}), bf16[1,2,2048,768]{3,2,1,0:T(8,128)(2,1)}) %all-gather.3.cloned.1.call-update) | async-done | bytes 6291472 | tf_op jit(solution)/shard_map/all_gather | solution.py:92
  219.6 4.7 %fusion.5 = f32[768,768]{0,1:T(8,128)S(1)} fusion(bf16[768,2048]{1,0:T(8,128)(2,1)S(1)} %bitcast.106, bf16[1,2,2048,768]{3,2,1,0:T(8,128)(2,1)} %all-gather.3.cloned.1.call-done), kind=kOutput, calls=%fused_computation.21 | convolution fusion | flops 2415919104 | bytes 8650752 | tf_op jit(solution)/shard_map/dot_general | solution.py:106
  224.3 3.5 multiply_convert_fusion.2
  227.8 5.9 %convolution_convert_fusion.1 = bf16[2048,768]{0,1:T(8,128)(2,1)S(1)} fusion(bf16[768,768]{0,1:T(8,128)(2,1)S(1)} %get-tuple-element.19, bf16[768,2048]{1,0:T(8,128)(2,1)} %bitcast.27), kind=kOutput, calls=%fused_computation.10 | convolution fusion | flops 2417491968 | bytes 7471104 | tf_op jit(solution)/shard_map/dot_general | solution.py:53
  233.8 6.3 %convolution_convert_fusion = bf16[2048,1536]{0,1:T(8,128)(2,1)S(1)} fusion(bf16[768,2048]{1,0:T(8,128)(2,1)S(1)} %bitcast.108, bf16[768,768]{0,1:T(8,128)(2,1)S(1)} %get-tuple-element.18, bf16[768,768]{0,1:T(8,128)(2,1)S(1)} %get-tuple-element.17), kind=kOutput, calls=%fused_computation.6 | convolution fusion | flops 4839702528 | bytes 11796480 | tf_op jit(solution)/shard_map/dot_general | solution.py:53
  240.1 11.6 %pad_maximum_fusion = bf16[2048,2304]{0,1:T(8,128)(2,1)} fusion(bf16[2048,768]{0,1:T(8,128)(2,1)S(1)} %convolution_convert_fusion.1, bf16[2048,1536]{0,1:T(8,128)(2,1)S(1)} %convolution_convert_fusion), kind=kLoop, calls=%fused_computation.5 | loop fusion | flops 18874368 | bytes 18874368 | tf_op jit(solution)/shard_map/concatenate | solution.py:152
  251.7 5.1 %fusion.4 = f32[768,2048]{1,0:T(8,128)S(1)} fusion(bf16[768,768]{0,1:T(8,128)(2,1)} %copy-done.17, bf16[1,2,2048,768]{3,2,1,0:T(8,128)(2,1)} %all-gather.3.cloned.1.call-done), kind=kOutput, calls=%fused_computation.20 | convolution fusion | flops 2415919104 | bytes 10616832 | tf_op jit(solution)/shard_map/dot_general | solution.py:59
  256.8 4.1 add_convert_fusion
  261.0 5.7 %all-to-all-start.3 = ((bf16[16,48,2048]{2,1,0:T(8,128)(2,1)}), bf16[16,48,2048]{2,1,0:T(8,128)(2,1)S(1)}, u32[]{:S(2)}, u32[]{:S(2)}) async-start(bf16[16,48,2048]{2,1,0:T(8,128)(2,1)} %bitcast.109), calls=%async_computation.3 | async-start | bytes 6291456 | tf_op jit(solution)/shard_map/all_to_all | solution.py:138
  266.7 6.6 %convolution_convert_fusion.2 = bf16[768,2048]{1,0:T(8,128)(2,1)} fusion(bf16[768,768]{0,1:T(8,128)(2,1)} %copy-done.19, bf16[1,768,2048]{2,1,0:T(8,128)(2,1)} %all-gather.5.cloned.1.call-done), kind=kOutput, calls=%fused_computation.11 | convolution fusion | flops 2417491968 | bytes 7471104 | tf_op jit(solution)/shard_map/dot_general | solution.py:109
  273.3 33.9 %all-to-all-done.3 = bf16[16,48,2048]{2,1,0:T(8,128)(2,1)S(1)} async-done(((bf16[16,48,2048]{2,1,0:T(8,128)(2,1)}), bf16[16,48,2048]{2,1,0:T(8,128)(2,1)S(1)}, u32[]{:S(2)}, u32[]{:S(2)}) %all-to-all-start.3) | async-done | bytes 3145760 | tf_op jit(solution)/shard_map/all_to_all | solution.py:138
  307.2 7.2 %all-to-all-start.1 = ((bf16[16,48,2048]{2,1,0:T(8,128)(2,1)}), bf16[16,48,2048]{2,1,0:T(8,128)(2,1)}, u32[]{:S(2)}, u32[]{:S(2)}) async-start(bf16[16,48,2048]{2,1,0:T(8,128)(2,1)} %bitcast.105), calls=%async_computation.1 | async-start | bytes 6291456 | tf_op jit(solution)/shard_map/all_to_all | solution.py:112
  314.5 2.5 convert_element_type.94
  317.0 2.9 collective-permute-start.2
  319.9 1.0 convert_element_type.97
  320.9 0.8 convert_element_type.101
  321.8 2.9 collective-permute-start.4
  324.6 0.8 convert_element_type.103
  325.6 3.3 gather_fusion.3
  328.9 30.2 %all-to-all-done.1 = bf16[16,48,2048]{2,1,0:T(8,128)(2,1)} async-done(((bf16[16,48,2048]{2,1,0:T(8,128)(2,1)}), bf16[16,48,2048]{2,1,0:T(8,128)(2,1)}, u32[]{:S(2)}, u32[]{:S(2)}) %all-to-all-start.1) | async-done | bytes 3145760 | tf_op jit(solution)/shard_map/all_to_all | solution.py:112
  359.1 7.7 %gather_fusion.2 = bf16[512,2048]{1,0:T(8,128)(2,1)} fusion(bf16[768,2048]{1,0:T(8,128)(2,1)} %bitcast.25, s32[1024]{0:T(1024)S(1)} %pad_clamp_fusion.1), kind=kCustom, calls=%fused_computation.clone | custom fusion | bytes 4196352 | tf_op jit(solution)/shard_map/jit(_take)/gather | solution.py:119
  366.8 4.9 %broadcast_select_fusion = (bf16[512,2048]{1,0:T(8,128)(2,1)}, f32[512,2048]{1,0:T(8,128)}) fusion(bf16[512,2048]{1,0:T(8,128)(2,1)S(1)} %copy-done.2, pred[512]{0:T(512)(128)(4,1)S(1)} %get-tuple-element.15, bf16[512,2048]{1,0:T(8,128)(2,1)} %gather_fusion.2), kind=kLoop, calls=%fused_computation.32 | loop fusion | flops 3145728 | bytes 10486272 | tf_op jit(solution)/shard_map/jit(_take)/select_n | solution.py:145
  371.7 5.2 %reshape.153 = f32[128,4,2048]{2,1,0:T(4,128)} reshape(f32[512,2048]{1,0:T(8,128)} %get-tuple-element.27) | data formatting | bytes 8388608 | tf_op jit(solution)/shard_map/convert_element_type | solution.py:122
  376.9 2.9 reshape.151
  379.8 3.9 reduce_sum.45
  383.7 6.2 %multiply_reduce_fusion = bf16[128,2048]{1,0:T(8,128)(2,1)} fusion(f32[128,4,2048]{2,1,0:T(4,128)} %reshape.153, f32[128,4]{1,0:T(8,128)S(1)} %copy.21), kind=kLoop, calls=%fused_computation.9 | loop fusion | flops 1835008 | bytes 4720640 | tf_op jit(solution)/shard_map/reduce_sum | solution.py:122
  389.9 52.0 %reduce-scatter.2.cloned.1.call-done = bf16[256,2304]{0,1:T(8,128)(2,1)} async-done(((bf16[2048,2304]{0,1:T(8,128)(2,1)}), bf16[256,2304]{0,1:T(8,128)(2,1)}) %reduce-scatter.2.cloned.1.call-update) | async-done | bytes 1179664 | tf_op jit(solution)/shard_map/reduce_scatter | solution.py:151
  441.9 1.2 slice.52
  443.2 1.6 copy.28
  444.8 0.2 convert_element_type.96
  445.0 0.9 copy-done.3
  445.9 0.5 copy-done.5
  446.4 4.7 %subtract_convert_fusion = (bf16[1,2,256,768]{3,2,1,0:T(8,128)(2,1)}, f32[1,2,256,768]{3,2,1,0:T(8,128)}, f32[1,2,256,768]{3,2,1,0:T(8,128)}) fusion(bf16[1,2,256,768]{3,2,1,0:T(8,128)(2,1)S(1)} %copy-done.3, f32[256,2,768]{2,0,1:T(8,128)} %copy.28, f32[1,2,256,768]{3,2,1,0:T(8,128)S(1)} %copy-done.5, bf16[1,2,256,768]{3,2,1,0:T(8,128)(2,1)} %collective-permute-done.2, ...), kind=kLoop, calls=%fused_computation.37 | loop fusion | flops 7077888 | bytes 11010049 | tf_op jit(solution)/shard_map/convert_element_type | solution.py:31
  451.2 2.9 subtract_convert_fusion.1
  (77 shorter events, 1.4 us)
Async XLA Ops:
  7.2 77.6 %copy-start = (bf16[128,2048]{1,0:T(8,128)(2,1)S(1)}, bf16[128,2048]{1,0:T(8,128)(2,1)}, u32[]{:S(2)}) copy-start(bf16[128,2048]{1,0:T(8,128)(2,1)} %param.13) | copy-start | bytes 1572868
  7.2 125.8 %all-gather.5.cloned.1.call-start = ((), (), s32[]{:S(2)}) async-start(), calls=%async_computation.6 | async-start | bytes 3538944 | tf_op jit(solution)/shard_map/all_gather | solution.py:93
  7.2 12.6 %collective-permute-start.1 = (bf16[1,768,256]{2,1,0:T(8,128)(2,1)}, bf16[1,768,256]{2,1,0:T(8,128)(2,1)S(1)}, u32[]{:S(2)}, u32[]{:S(2)}) collective-permute-start(bf16[1,768,256]{2,1,0:T(8,128)(2,1)} %param.18), channel_id=1, source_target_pairs={{64,0},{72,8},{80,16},{88,24},{96,32},{104,40},{112,48},{120,56},{... | collective-permute-start | bytes 1179656 | tf_op jit(solution)/shard_map/ppermute | solution.py:17
  13.0 28.1 %copy-start.14 = (s32[128,4]{0,1:T(4,128)S(1)}, s32[128,4]{0,1:T(4,128)}, u32[]{:S(2)}) copy-start(s32[128,4]{0,1:T(4,128)} %param.14) | copy-start | bytes 6148
  13.0 28.4 %copy-start.12 = (bf16[128,2048]{1,0:T(8,128)(2,1)S(1)}, bf16[128,2048]{1,0:T(8,128)(2,1)}, u32[]{:S(2)}) copy-start(bf16[128,2048]{1,0:T(8,128)(2,1)} %param.23) | copy-start | bytes 1572868
  20.6 198.9 %all-gather.3.cloned.1.call-start = ((), (), s32[]{:S(2)}) async-start(), calls=%async_computation.5 | async-start | bytes 7077888 | tf_op jit(solution)/shard_map/all_gather | solution.py:92
  20.7 19.4 %collective-permute-start = (bf16[1,2,256,768]{3,2,1,0:T(8,128)(2,1)}, bf16[1,2,256,768]{3,2,1,0:T(8,128)(2,1)S(1)}, u32[]{:S(2)}, u32[]{:S(2)}) collective-permute-start(bf16[1,2,256,768]{3,2,1,0:T(8,128)(2,1)} %param.17), channel_id=1, source_target_pairs={{64,0},{72,8},{80,16},{88,24},{96,32},{104,40},{112,48},{120,56},{... | collective-permute-start | bytes 2359304 | tf_op jit(solution)/shard_map/ppermute | solution.py:17
  44.5 5.3 %copy-start.15 = (f32[128,4]{0,1:T(4,128)S(1)}, f32[128,4]{0,1:T(4,128)}, u32[]{:S(2)}) copy-start(f32[128,4]{0,1:T(4,128)} %param.15) | copy-start | bytes 6148
  44.5 5.6 %copy-start.13 = (s32[16]{0:T(128)S(1)}, s32[16]{0:T(128)}, u32[]{:S(2)}) copy-start(s32[16]{0:T(128)} %param.16) | copy-start | bytes 196
  75.5 49.0 %all-to-all-start.2 = ((bf16[16,48,2048]{2,1,0:T(8,128)(2,1)}), bf16[16,48,2048]{2,1,0:T(8,128)(2,1)}, u32[]{:S(2)}, u32[]{:S(2)}) async-start(bf16[16,48,2048]{2,1,0:T(8,128)(2,1)} %select_select_fusion), calls=%async_computation.2 | async-start | bytes 6291456 | tf_op jit(solution)/shard_map/all_to_all | solution.py:129
  124.6 48.1 %all-to-all-start = ((bf16[16,48,2048]{2,1,0:T(8,128)(2,1)}), bf16[16,48,2048]{2,1,0:T(8,128)(2,1)S(1)}, u32[]{:S(2)}, u32[]{:S(2)}) async-start(bf16[16,48,2048]{2,1,0:T(8,128)(2,1)} %select_select_fusion.1), calls=%async_computation | async-start | bytes 6291456 | tf_op jit(solution)/shard_map/all_to_all | solution.py:102
  132.6 309.3 %reduce-scatter.2.cloned.1.call-start = ((), (), s32[]{:S(2)}) async-start(), calls=%async_computation.7 | async-start | bytes 10616832 | tf_op jit(solution)/shard_map/reduce_scatter | solution.py:151
  219.6 4.7 %copy-start.16 = (bf16[1,2,2048,768]{3,2,1,0:T(8,128)(2,1)S(1)}, bf16[1,2,2048,768]{3,2,1,0:T(8,128)(2,1)}, u32[]{:S(2)}) copy-start(bf16[1,2,2048,768]{3,2,1,0:T(8,128)(2,1)} %all-gather.3.cloned.1.call-done) | copy-start | bytes 18874372
  219.6 4.7 %copy-start.18 = (f32[768,768]{0,1:T(8,128)S(1)}, f32[768,768]{0,1:T(8,128)}, u32[]{:S(2)}) copy-start(f32[768,768]{0,1:T(8,128)} %fusion) | copy-start | bytes 7077892
  227.8 5.9 %copy-start.19 = (bf16[768,768]{0,1:T(8,128)(2,1)}, bf16[768,768]{0,1:T(8,128)(2,1)S(1)}, u32[]{:S(2)}) copy-start(bf16[768,768]{0,1:T(8,128)(2,1)S(1)} %get-tuple-element.19) | copy-start | bytes 3538948
  227.8 5.9 %copy-start.17 = (bf16[768,768]{0,1:T(8,128)(2,1)}, bf16[768,768]{0,1:T(8,128)(2,1)S(1)}, u32[]{:S(2)}) copy-start(bf16[768,768]{0,1:T(8,128)(2,1)S(1)} %get-tuple-element.18) | copy-start | bytes 3538948
  227.8 5.9 %copy-start.20 = (bf16[768,768]{0,1:T(8,128)(2,1)}, bf16[768,768]{0,1:T(8,128)(2,1)S(1)}, u32[]{:S(2)}) copy-start(bf16[768,768]{0,1:T(8,128)(2,1)S(1)} %get-tuple-element.17) | copy-start | bytes 3538948
  251.7 5.1 %slice-start = ((s8[6291456]{0:T(1024)(128)(4,1)}), s8[2097152]{0:T(1024)(128)(4,1)S(1)}, s32[]{:S(2)}) async-start(s8[6291456]{0:T(1024)(128)(4,1)} %bitcast.112), calls=%async_computation.8 | async-start | bytes 4194304
  251.7 5.1 %slice-start.1 = ((s8[6291456]{0:T(1024)(128)(4,1)}), s8[4194304]{0:T(1024)(128)(4,1)S(1)}, s32[]{:S(2)}) async-start(s8[6291456]{0:T(1024)(128)(4,1)} %bitcast.112), calls=%async_computation.9 | async-start | bytes 8388608
  251.7 5.1 %copy-start.21 = (bf16[768,768]{0,1:T(8,128)(2,1)S(1)}, bf16[768,768]{0,1:T(8,128)(2,1)}, u32[]{:S(2)}) copy-start(bf16[768,768]{0,1:T(8,128)(2,1)} %copy-done.20) | copy-start | bytes 3538948
  261.0 46.3 %all-to-all-start.3 = ((bf16[16,48,2048]{2,1,0:T(8,128)(2,1)}), bf16[16,48,2048]{2,1,0:T(8,128)(2,1)S(1)}, u32[]{:S(2)}, u32[]{:S(2)}) async-start(bf16[16,48,2048]{2,1,0:T(8,128)(2,1)} %bitcast.109), calls=%async_computation.3 | async-start | bytes 6291456 | tf_op jit(solution)/shard_map/all_to_all | solution.py:138
  307.2 51.9 %all-to-all-start.1 = ((bf16[16,48,2048]{2,1,0:T(8,128)(2,1)}), bf16[16,48,2048]{2,1,0:T(8,128)(2,1)}, u32[]{:S(2)}, u32[]{:S(2)}) async-start(bf16[16,48,2048]{2,1,0:T(8,128)(2,1)} %bitcast.105), calls=%async_computation.1 | async-start | bytes 6291456 | tf_op jit(solution)/shard_map/all_to_all | solution.py:112
  314.4 5.4 %copy-start.6 = (f32[1,2,256,768]{3,2,1,0:T(8,128)S(1)}, f32[1,2,256,768]{3,2,1,0:T(8,128)}, u32[]{:S(2)}) copy-start(f32[1,2,256,768]{3,2,1,0:T(8,128)} %param.20) | copy-start | bytes 4718596
  314.4 6.5 %copy-start.8 = (f32[1,768,256]{2,1,0:T(8,128)S(1)}, f32[1,768,256]{2,1,0:T(8,128)}, u32[]{:S(2)}) copy-start(f32[1,768,256]{2,1,0:T(8,128)} %param.21) | copy-start | bytes 2359300
  314.5 10.2 %copy-start.10 = (f32[1,768,256]{2,1,0:T(8,128)S(1)}, f32[1,768,256]{2,1,0:T(8,128)}, u32[]{:S(2)}) copy-start(f32[1,768,256]{2,1,0:T(8,128)} %param.22) | copy-start | bytes 2359300
  317.0 128.0 %collective-permute-start.2 = (bf16[1,2,256,768]{3,2,1,0:T(8,128)(2,1)}, bf16[1,2,256,768]{3,2,1,0:T(8,128)(2,1)}, u32[]{:S(2)}, u32[]{:S(2)}) collective-permute-start(bf16[1,2,256,768]{3,2,1,0:T(8,128)(2,1)} %convert_element_type.94), channel_id=1, source_target_pairs={{64,0},{72,8},{80,16},{88,24},{96,32},{104,40},{112,48},{120,56},{... | collective-permute-start | bytes 2359304 | tf_op jit(solution)/shard_map/ppermute | solution.py:17
  320.8 124.2 %collective-permute-start.3 = (bf16[1,2,256,768]{3,2,1,0:T(8,128)(2,1)}, bf16[1,2,256,768]{3,2,1,0:T(8,128)(2,1)}, u32[]{:S(2)}, u32[]{:S(2)}) collective-permute-start(bf16[1,2,256,768]{3,2,1,0:T(8,128)(2,1)} %convert_element_type.97), channel_id=1, source_target_pairs={{64,0},{72,8},{80,16},{88,24},{96,32},{104,40},{112,48},{120,56},{... | collective-permute-start | bytes 2359304 | tf_op jit(solution)/shard_map/ppermute | solution.py:17
  321.8 129.4 %collective-permute-start.4 = (bf16[1,768,256]{2,1,0:T(8,128)(2,1)}, bf16[1,768,256]{2,1,0:T(8,128)(2,1)}, u32[]{:S(2)}, u32[]{:S(2)}) collective-permute-start(bf16[1,768,256]{2,1,0:T(8,128)(2,1)} %convert_element_type.101), channel_id=1, source_target_pairs={{64,0},{72,8},{80,16},{88,24},{96,32},{104,40},{112,48},{120,56},{... | collective-permute-start | bytes 1179656 | tf_op jit(solution)/shard_map/ppermute | solution.py:17
  325.4 125.8 %collective-permute-start.5 = (bf16[1,768,256]{2,1,0:T(8,128)(2,1)}, bf16[1,768,256]{2,1,0:T(8,128)(2,1)}, u32[]{:S(2)}, u32[]{:S(2)}) collective-permute-start(bf16[1,768,256]{2,1,0:T(8,128)(2,1)} %convert_element_type.103), channel_id=1, source_target_pairs={{64,0},{72,8},{80,16},{88,24},{96,32},{104,40},{112,48},{120,56},{... | collective-permute-start | bytes 1179656 | tf_op jit(solution)/shard_map/ppermute | solution.py:17
  359.1 7.7 %copy-start.2 = (bf16[512,2048]{1,0:T(8,128)(2,1)S(1)}, bf16[512,2048]{1,0:T(8,128)(2,1)}, u32[]{:S(2)}) copy-start(bf16[512,2048]{1,0:T(8,128)(2,1)} %gather_fusion.3) | copy-start | bytes 6291460
  443.1 1.6 copy-start.4
  444.8 1.1 copy-start.3
  444.8 1.7 copy-start.5
  445.0 6.2 %copy-start.7 = (bf16[1,768,256]{2,1,0:T(8,128)(2,1)S(1)}, bf16[1,768,256]{2,1,0:T(8,128)(2,1)}, u32[]{:S(2)}) copy-start(bf16[1,768,256]{2,1,0:T(8,128)(2,1)} %broadcast_select_fusion.2) | copy-start | bytes 1179652
  445.0 6.2 %copy-start.9 = (f32[1,768,256]{2,1,0:T(8,128)S(1)}, f32[1,768,256]{2,1,0:T(8,128)}, u32[]{:S(2)}) copy-start(f32[1,768,256]{2,1,0:T(8,128)} %param.21) | copy-start | bytes 2359300
  445.0 6.2 %copy-start.11 = (f32[1,768,256]{2,1,0:T(8,128)S(1)}, f32[1,768,256]{2,1,0:T(8,128)}, u32[]{:S(2)}) copy-start(f32[1,768,256]{2,1,0:T(8,128)} %param.22) | copy-start | bytes 2359300
  446.4 7.7 %copy-start.1 = (bf16[128,2048]{1,0:T(8,128)(2,1)S(1)}, bf16[128,2048]{1,0:T(8,128)(2,1)}, u32[]{:S(2)}) copy-start(bf16[128,2048]{1,0:T(8,128)(2,1)} %param.13) | copy-start | bytes 1572868
Sparse Core Ops, SparseCore 0:
  20.8 70.2 all-gather.4
  93.8 125.6 all-gather.2
  251.8 190.0 reduce-scatter.1
where the time goes:
time: 467 us; the launch traced here: 461 us
  waiting for transfers between devices  251 us (54%)
  other arithmetic  63.2 us (14%)
  local copies, waits for them, and re-layouts  45 us (10%)
  matrix products  43.3 us (9%)
  starting transfers between devices  43.2 us (9%)
  between operations  15.1 us (3%)
    reduce_scatter x1, waiting for transfers between devices, body(): lax.psum_scatter(jnp.concatenate([contract_rows(rows_x, grad_both), contr...  52 us
    all_gather x1, waiting for transfers between devices, body(): lax.all_gather(w_in, 'shard', axis=2, tiled=True)  46.9 us
    all_to_all x1, waiting for transfers between devices, body(): lax.all_to_all(entry_grads.reshape(groups, capacity, width), 'expert', sp...  33.9 us
    all_to_all x1, waiting for transfers between devices, body(): lax.all_to_all(send_rows, 'expert', split_axis=0, concat_axis=0, tiled=True)  32.7 us
    all_to_all x1, waiting for transfers between devices, body(): lax.all_to_all(send_grads, 'expert', split_axis=0, concat_axis=0, tiled=T...  32.1 us
    all_to_all x1, waiting for transfers between devices, body(): lax.all_to_all(expert_out.reshape(groups, capacity, width), 'expert', spl...  30.2 us
    ppermute x6, waiting for transfers between devices, shifted(): return lax.ppermute(block, axis, route)  23.2 us
    dot_general x3, matrix products, contract_cols(): lax.dot_general(left, right, (((1,), (1,)), ((), ())), preferred_element_...  16.2 us
  transfers between devices with their start and end apart: 13, of which 8 were waited for; matrix products, arithmetic and copies ran while one was open for 25% of the time, Pallas kernels for 0%

commit v1 on v0

--- a/solution.py
+++ b/solution.py
@@ -89,7 +89,9 @@
         for moved, owned in zip(moved_states, (m_in, v_in, m_down, v_down))
     )
     in_full, down_full = (
-        lax.all_gather(w_in, "shard", axis=2, tiled=True),
+        jnp.concatenate(
+            lax.all_to_all(jnp.stack([w_in] * lax.axis_size("shard")), "shard", 0, 0), axis=2
+        ),
         lax.all_gather(w_down, "shard", axis=2, tiled=True),
     )
     gate_weight = in_full[0, 0]

time: 467 us -> 512 us (1.096)
  waiting for transfers between devices: 251 us -> 284 us
  local copies, waits for them, and re-layouts: 45 us -> 53.9 us
    all_to_all x0 -> x1, waiting for transfers between devices: none -> 49 us  [body(): lax.all_to_all(jnp.stack([w_in] * lax.axis_size('shard')), 'shard', 0, 0)]
    all_gather x1 -> x0, waiting for transfers between devices: 46.9 us -> none  [body(): lax.all_gather(w_in, 'shard', axis=2, tiled=True)]
    ppermute x6, waiting for transfers between devices: 23.2 us -> 66.7 us  [shifted(): return lax.ppermute(block, axis, route)]
    all_to_all x1, waiting for transfers between devices: 32.7 us -> 0.01 us  [body(): lax.all_to_all(send_rows, 'expert', split_axis=0, concat_axis=0, tiled=True)]
    all_gather x1, waiting for transfers between devices: 0.02 us -> 19.3 us  [body(): lax.all_gather(w_down, 'shard', axis=2, tiled=True)]
    all_to_all x0 -> x1, starting transfers between devices: none -> 7.17 us  [body(): lax.all_to_all(jnp.stack([w_in] * lax.axis_size('shard')), 'shard', 0, 0)]
    all_to_all x1, waiting for transfers between devices: 32.1 us -> 26.3 us  [body(): lax.all_to_all(send_grads, 'expert', split_axis=0, concat_axis=0, tiled=T...]
    reduce_scatter x1, waiting for transfers between devices: 52 us -> 57.7 us  [body(): lax.psum_scatter(jnp.concatenate([contract_rows(rows_x, grad_both), contr...]
  transfers between devices with their start and end apart: 13 -> 13, of which waited for: 8 -> 8; matrix products, arithmetic and copies ran while one was open for 25% -> 20% of each run, Pallas kernels for 0% -> 0%
where the time goes in v1:
time: 512 us; the launch traced here: 505 us
  waiting for transfers between devices  284 us (55%)
  other arithmetic  62.7 us (12%)
  local copies, waits for them, and re-layouts  53.9 us (11%)
  matrix products  48.2 us (9%)
  starting transfers between devices  40.1 us (8%)
  between operations  15.6 us (3%)
    ppermute x6, waiting for transfers between devices, shifted(): return lax.ppermute(block, axis, route)  66.7 us
    reduce_scatter x1, waiting for transfers between devices, body(): lax.psum_scatter(jnp.concatenate([contract_rows(rows_x, grad_both), contr...  57.7 us
    all_to_all x1, waiting for transfers between devices, body(): lax.all_to_all(jnp.stack([w_in] * lax.axis_size('shard')), 'shard', 0, 0)  49 us
    all_to_all x1, waiting for transfers between devices, body(): lax.all_to_all(entry_grads.reshape(groups, capacity, width), 'expert', sp...  37.8 us
    all_to_all x1, waiting for transfers between devices, body(): lax.all_to_all(expert_out.reshape(groups, capacity, width), 'expert', spl...  27.4 us
    all_to_all x1, waiting for transfers between devices, body(): lax.all_to_all(send_grads, 'expert', split_axis=0, concat_axis=0, tiled=T...  26.3 us
    all_gather x1, waiting for transfers between devices, body(): lax.all_gather(w_down, 'shard', axis=2, tiled=True)  19.3 us
    dot_general x3, matrix products, contract_cols(): lax.dot_general(left, right, (((1,), (1,)), ((), ())), preferred_element_...  15.8 us
  transfers between devices with their start and end apart: 13, of which 8 were waited for; matrix products, arithmetic and copies ran while one was open for 20% of the time, Pallas kernels for 0%

profile of v1, /device:TPU:1, one launch (start us, length us, event | category | flops | bytes accessed | tf_op | source)
XLA Modules:
  0.0 504.8 jit_solution(12579448943334867809)
XLA Ops:
  7.2 0.8 copy.31
  8.1 0.1 eq.35
  8.2 1.9 fusion.28
  10.2 10.8 %select_multiply_fusion = s32[128,4]{0,1:T(4,128)S(1)} fusion(s32[128,4]{0,1:T(4,128)} %param.14, s32[]{:T(128)} %bitcast, s32[]{:T(128)} %bitcast.1, s32[]{:T(128)} %bitcast.2, s32[]{:T(128)} %bitcast.3, s32[]{:T(128)} %bitcast.4, s32[]{:T(128)} %bitcast.5, s32[]{:T(128)} %bitcast.6, s32[]{:T(128)} %bitcast.7, s32[]{:T(128)} %bitcast.8, s32[]{:T(128)} %bitcast.9, ...), kind=kLoop, calls=%fused_computation.70 | loop fusion | flops 17408 | bytes 4160 | tf_op jit(solution)/shard_map/mul | solution.py:40
  21.0 0.1 copy.30
  21.2 1.2 reduce-window.6
  22.4 0.2 slice_reduce_fusion
  22.8 2.4 scatter_custom_fusion
  25.5 4.3 gather_fusion
  29.7 3.3 select_select_fusion.1
  33.0 7.5 %all-to-all-start = ((bf16[16,48,2048]{2,1,0:T(8,128)(2,1)}), bf16[16,48,2048]{2,1,0:T(8,128)(2,1)}, u32[]{:S(2)}, u32[]{:S(2)}) async-start(bf16[16,48,2048]{2,1,0:T(8,128)(2,1)} %select_select_fusion.1), calls=%async_computation | async-start | bytes 6291456 | tf_op jit(solution)/shard_map/all_to_all | solution.py:104
  40.5 3.0 collective-permute-start
  43.5 0.6 fusion.24
  44.8 55.6 %collective-permute-done = bf16[1,2,256,768]{3,2,1,0:T(8,128)(2,1)S(1)} collective-permute-done((bf16[1,2,256,768]{3,2,1,0:T(8,128)(2,1)S(1)}, bf16[1,2,256,768]{3,2,1,0:T(8,128)(2,1)S(1)}, u32[]{:S(2)}, u32[]{:S(2)}) %collective-permute-start) | collective-permute-done | bytes 786464 | tf_op jit(solution)/shard_map/ppermute | solution.py:17
  100.5 3.2 stack.2
  103.7 7.2 %all-to-all-start.1 = ((bf16[8,1,2,256,768]{4,3,2,1,0:T(8,128)(2,1)}), bf16[8,1,2,256,768]{4,3,2,1,0:T(8,128)(2,1)}, u32[]{:S(2)}, u32[]{:S(2)}) async-start(bf16[8,1,2,256,768]{4,3,2,1,0:T(8,128)(2,1)} %stack.2), calls=%async_computation.1 | async-start | bytes 12582912 | tf_op jit(solution)/shard_map/all_to_all | solution.py:93
  111.1 11.1 %collective-permute-done.1 = bf16[1,768,256]{2,1,0:T(8,128)(2,1)S(1)} collective-permute-done((bf16[1,768,256]{2,1,0:T(8,128)(2,1)S(1)}, bf16[1,768,256]{2,1,0:T(8,128)(2,1)S(1)}, u32[]{:S(2)}, u32[]{:S(2)}) %collective-permute-start.1) | collective-permute-done | bytes 393248 | tf_op jit(solution)/shard_map/ppermute | solution.py:17
  122.1 0.8 broadcast_select_fusion.2
  122.9 3.0 mul.160
  125.9 5.3 %mul.161 = f32[512,2048]{1,0:T(8,128)} reshape(f32[128,4,2048]{2,1,0:T(4,128)} %mul.160) | data formatting | bytes 8388608 | tf_op jit(solution)/shard_map/mul | solution.py:127
  131.2 0.1 copy.29
  131.6 2.5 multiply_convert_fusion
  134.1 4.3 gather_fusion.1
  138.4 3.3 select_select_fusion
  141.8 49.0 %all-to-all-done.1 = bf16[8,1,2,256,768]{4,3,2,1,0:T(8,128)(2,1)} async-done(((bf16[8,1,2,256,768]{4,3,2,1,0:T(8,128)(2,1)}), bf16[8,1,2,256,768]{4,3,2,1,0:T(8,128)(2,1)}, u32[]{:S(2)}, u32[]{:S(2)}) %all-to-all-start.1) | async-done | bytes 6291488 | tf_op jit(solution)/shard_map/all_to_all | solution.py:93
  190.8 4.4 all-to-all-start.3
  195.2 0.5 reduce-scatter.2.cloned.1.call-start
  195.7 3.4 copy.35
  199.1 8.4 %fusion.4 = f32[768,768]{0,1:T(8,128)} fusion(bf16[768,2048]{1,0:T(8,128)(2,1)} %bitcast.20, bf16[1,2,2048,768]{3,2,1,0:T(8,128)(2,1)S(1)} %bitcast.109), kind=kOutput, calls=%fused_computation.20 | convolution fusion | flops 2415919104 | bytes 8650752 | tf_op jit(solution)/shard_map/dot_general | solution.py:107
  207.5 6.1 %fusion.5 = f32[768,768]{0,1:T(8,128)} fusion(bf16[768,2048]{1,0:T(8,128)(2,1)} %bitcast.20, bf16[1,2,2048,768]{3,2,1,0:T(8,128)(2,1)S(1)} %bitcast.110), kind=kOutput, calls=%fused_computation.21 | convolution fusion | flops 2415919104 | bytes 8650752 | tf_op jit(solution)/shard_map/dot_general | solution.py:108
  213.6 26.3 %all-to-all-done.3 = bf16[16,48,2048]{2,1,0:T(8,128)(2,1)S(1)} async-done(((bf16[16,48,2048]{2,1,0:T(8,128)(2,1)}), bf16[16,48,2048]{2,1,0:T(8,128)(2,1)S(1)}, u32[]{:S(2)}, u32[]{:S(2)}) %all-to-all-start.3) | async-done | bytes 3145760 | tf_op jit(solution)/shard_map/all_to_all | solution.py:131
  239.9 19.3 %all-gather.2.cloned.1.call-done = bf16[1,768,2048]{2,1,0:T(8,128)(2,1)} async-done(((bf16[1,768,256]{2,1,0:T(8,128)(2,1)}), bf16[1,768,2048]{2,1,0:T(8,128)(2,1)}) %all-gather.2.cloned.1.call-update) | async-done | bytes 3145744 | tf_op jit(solution)/shard_map/all_gather | solution.py:95
  259.2 6.7 %multiply_convert_fusion.1 = (bf16[768,768]{0,1:T(8,128)(2,1)S(1)}, bf16[768,768]{0,1:T(8,128)(2,1)S(1)}, bf16[768,768]{0,1:T(8,128)(2,1)S(1)}) fusion(f32[768,768]{0,1:T(8,128)} %fusion.4, f32[768,768]{0,1:T(8,128)} %fusion.5, bf16[768,2048]{1,0:T(8,128)(2,1)S(1)} %bitcast.117, bf16[1,768,2048]{2,1,0:T(8,128)(2,1)} %all-gather.2.cloned.1.call-done), kind=kOutput, calls=%fused_computation.26 | convolution fusion | flops 2424766464 | bytes 14548992 | tf_op jit(solution)/shard_map/dot_general | solution.py:59
  265.9 3.0 convolution_convert_fusion.1
  268.9 8.3 %convolution_convert_fusion = bf16[2048,1536]{0,1:T(8,128)(2,1)S(1)} fusion(bf16[768,2048]{1,0:T(8,128)(2,1)} %bitcast.20, bf16[768,768]{0,1:T(8,128)(2,1)S(1)} %get-tuple-element.17, bf16[768,768]{0,1:T(8,128)(2,1)S(1)} %get-tuple-element.18), kind=kOutput, calls=%fused_computation.6 | convolution fusion | flops 4839702528 | bytes 11796480 | tf_op jit(solution)/shard_map/dot_general | solution.py:53
  277.2 11.6 %pad_maximum_fusion = bf16[2048,2304]{0,1:T(8,128)(2,1)} fusion(bf16[2048,768]{0,1:T(8,128)(2,1)S(1)} %convolution_convert_fusion.1, bf16[2048,1536]{0,1:T(8,128)(2,1)S(1)} %convolution_convert_fusion), kind=kLoop, calls=%fused_computation.5 | loop fusion | flops 18874368 | bytes 18874368 | tf_op jit(solution)/shard_map/concatenate | solution.py:154
  288.9 5.1 %fusion.3 = f32[768,2048]{1,0:T(8,128)S(1)} fusion(bf16[768,768]{0,1:T(8,128)(2,1)} %copy-done.20, bf16[1,2,2048,768]{3,2,1,0:T(8,128)(2,1)} %bitcast.111), kind=kOutput, calls=%fused_computation.19 | convolution fusion | flops 2415919104 | bytes 10616832 | tf_op jit(solution)/shard_map/dot_general | solution.py:59
  294.0 4.1 add_convert_fusion
  298.1 6.8 %all-to-all-start.4 = ((bf16[16,48,2048]{2,1,0:T(8,128)(2,1)}), bf16[16,48,2048]{2,1,0:T(8,128)(2,1)S(1)}, u32[]{:S(2)}, u32[]{:S(2)}) async-start(bf16[16,48,2048]{2,1,0:T(8,128)(2,1)} %bitcast.119), calls=%async_computation.4 | async-start | bytes 6291456 | tf_op jit(solution)/shard_map/all_to_all | solution.py:140
  304.9 6.6 %convolution_convert_fusion.2 = bf16[768,2048]{1,0:T(8,128)(2,1)} fusion(bf16[768,768]{0,1:T(8,128)(2,1)} %copy-done.21, bf16[1,768,2048]{2,1,0:T(8,128)(2,1)} %all-gather.2.cloned.1.call-done), kind=kOutput, calls=%fused_computation.11 | convolution fusion | flops 2417491968 | bytes 7471104 | tf_op jit(solution)/shard_map/dot_general | solution.py:111
  311.5 37.8 %all-to-all-done.4 = bf16[16,48,2048]{2,1,0:T(8,128)(2,1)S(1)} async-done(((bf16[16,48,2048]{2,1,0:T(8,128)(2,1)}), bf16[16,48,2048]{2,1,0:T(8,128)(2,1)S(1)}, u32[]{:S(2)}, u32[]{:S(2)}) %all-to-all-start.4) | async-done | bytes 3145760 | tf_op jit(solution)/shard_map/all_to_all | solution.py:140
  349.2 4.8 all-to-all-start.2
  354.1 2.5 convert_element_type.94
  356.6 2.9 collective-permute-start.2
  359.5 1.0 convert_element_type.97
  360.5 0.8 convert_element_type.101
  361.3 2.9 collective-permute-start.4
  364.2 0.8 convert_element_type.103
  365.2 3.3 gather_fusion.3
  368.5 27.4 %all-to-all-done.2 = bf16[16,48,2048]{2,1,0:T(8,128)(2,1)} async-done(((bf16[16,48,2048]{2,1,0:T(8,128)(2,1)}), bf16[16,48,2048]{2,1,0:T(8,128)(2,1)}, u32[]{:S(2)}, u32[]{:S(2)}) %all-to-all-start.2) | async-done | bytes 3145760 | tf_op jit(solution)/shard_map/all_to_all | solution.py:114
  395.9 7.7 %gather_fusion.2 = bf16[512,2048]{1,0:T(8,128)(2,1)} fusion(bf16[768,2048]{1,0:T(8,128)(2,1)} %bitcast.29, s32[1024]{0:T(1024)S(1)} %pad_clamp_fusion.1), kind=kCustom, calls=%fused_computation.clone | custom fusion | bytes 4196352 | tf_op jit(solution)/shard_map/jit(_take)/gather | solution.py:121
  403.6 4.8 broadcast_select_fusion
  408.4 5.3 %reshape.164 = f32[128,4,2048]{2,1,0:T(4,128)} reshape(f32[512,2048]{1,0:T(8,128)} %get-tuple-element.27) | data formatting | bytes 8388608 | tf_op jit(solution)/shard_map/convert_element_type | solution.py:124
  413.7 3.0 reshape.162
  416.7 3.9 reduce_sum.45
  420.6 6.2 %multiply_reduce_fusion = bf16[128,2048]{1,0:T(8,128)(2,1)} fusion(f32[128,4,2048]{2,1,0:T(4,128)} %reshape.164, f32[128,4]{1,0:T(8,128)S(1)} %copy.29), kind=kLoop, calls=%fused_computation.9 | loop fusion | flops 1835008 | bytes 4720640 | tf_op jit(solution)/shard_map/reduce_sum | solution.py:124
  426.8 57.7 %reduce-scatter.2.cloned.1.call-done = bf16[256,2304]{0,1:T(8,128)(2,1)} async-done(((bf16[2048,2304]{0,1:T(8,128)(2,1)}), bf16[256,2304]{0,1:T(8,128)(2,1)}) %reduce-scatter.2.cloned.1.call-update) | async-done | bytes 1179664 | tf_op jit(solution)/shard_map/reduce_scatter | solution.py:153
  484.5 1.3 slice.52
  485.8 1.6 copy.37
  487.5 0.2 convert_element_type.96
  487.7 1.2 copy-done.5
  488.9 0.5 copy-done.7
  489.3 5.2 %subtract_convert_fusion = (bf16[1,2,256,768]{3,2,1,0:T(8,128)(2,1)}, f32[1,2,256,768]{3,2,1,0:T(8,128)}, f32[1,2,256,768]{3,2,1,0:T(8,128)}) fusion(bf16[1,2,256,768]{3,2,1,0:T(8,128)(2,1)} %copy-done.11, bf16[1,2,256,768]{3,2,1,0:T(8,128)(2,1)S(1)} %copy-done.10, pred[]{:T(512)S(6)} %ne.20, f32[256,2,768]{2,0,1:T(8,128)} %copy.37, ...), kind=kLoop, calls=%fused_computation.37 | loop fusion | flops 7471104 | bytes 11796481 | tf_op jit(solution)/shard_map/convert_element_type | solution.py:31
  494.6 2.9 subtract_convert_fusion.1
  (82 shorter events, 1.5 us)
Async XLA Ops:
  7.2 18.3 %copy-start = (bf16[128,2048]{1,0:T(8,128)(2,1)S(1)}, bf16[128,2048]{1,0:T(8,128)(2,1)}, u32[]{:S(2)}) copy-start(bf16[128,2048]{1,0:T(8,128)(2,1)} %param.13) | copy-start | bytes 1572868
  33.0 7.5 %copy-start.9 = (bf16[1,2,256,768]{3,2,1,0:T(8,128)(2,1)S(1)}, bf16[1,2,256,768]{3,2,1,0:T(8,128)(2,1)}, u32[]{:S(2)}) copy-start(bf16[1,2,256,768]{3,2,1,0:T(8,128)(2,1)} %param.17) | copy-start | bytes 2359300
  33.0 10.5 %copy-start.18 = (s32[16]{0:T(128)S(1)}, s32[16]{0:T(128)}, u32[]{:S(2)}) copy-start(s32[16]{0:T(128)} %param.16) | copy-start | bytes 196
  33.0 67.4 %all-to-all-start = ((bf16[16,48,2048]{2,1,0:T(8,128)(2,1)}), bf16[16,48,2048]{2,1,0:T(8,128)(2,1)}, u32[]{:S(2)}, u32[]{:S(2)}) async-start(bf16[16,48,2048]{2,1,0:T(8,128)(2,1)} %select_select_fusion.1), calls=%async_computation | async-start | bytes 6291456 | tf_op jit(solution)/shard_map/all_to_all | solution.py:104
  40.5 59.9 %collective-permute-start = (bf16[1,2,256,768]{3,2,1,0:T(8,128)(2,1)S(1)}, bf16[1,2,256,768]{3,2,1,0:T(8,128)(2,1)S(1)}, u32[]{:S(2)}, u32[]{:S(2)}) collective-permute-start(bf16[1,2,256,768]{3,2,1,0:T(8,128)(2,1)S(1)} %copy-done.9), channel_id=1, source_target_pairs={{64,0},{72,8},{80,16},{88,24},{96,32},{104,40},{112,48},{120,56},{... | collective-permute-start | bytes 2359304 | tf_op jit(solution)/shard_map/ppermute | solution.py:17
  100.4 3.3 copy-start.11
  103.7 7.2 %copy-start.17 = (bf16[1,768,256]{2,1,0:T(8,128)(2,1)S(1)}, bf16[1,768,256]{2,1,0:T(8,128)(2,1)}, u32[]{:S(2)}) copy-start(bf16[1,768,256]{2,1,0:T(8,128)(2,1)} %param.18) | copy-start | bytes 1179652
  103.7 19.2 %copy-start.16 = (bf16[128,2048]{1,0:T(8,128)(2,1)S(1)}, bf16[128,2048]{1,0:T(8,128)(2,1)}, u32[]{:S(2)}) copy-start(bf16[128,2048]{1,0:T(8,128)(2,1)} %param.23) | copy-start | bytes 1572868
  103.7 87.1 %all-to-all-start.1 = ((bf16[8,1,2,256,768]{4,3,2,1,0:T(8,128)(2,1)}), bf16[8,1,2,256,768]{4,3,2,1,0:T(8,128)(2,1)}, u32[]{:S(2)}, u32[]{:S(2)}) async-start(bf16[8,1,2,256,768]{4,3,2,1,0:T(8,128)(2,1)} %stack.2), calls=%async_computation.1 | async-start | bytes 12582912 | tf_op jit(solution)/shard_map/all_to_all | solution.py:93
  110.9 148.3 %all-gather.2.cloned.1.call-start = ((), (), s32[]{:S(2)}) async-start(), calls=%async_computation.6 | async-start | bytes 3538944 | tf_op jit(solution)/shard_map/all_gather | solution.py:95
  111.0 11.1 %collective-permute-start.1 = (bf16[1,768,256]{2,1,0:T(8,128)(2,1)S(1)}, bf16[1,768,256]{2,1,0:T(8,128)(2,1)S(1)}, u32[]{:S(2)}, u32[]{:S(2)}) collective-permute-start(bf16[1,768,256]{2,1,0:T(8,128)(2,1)S(1)} %copy-done.17), channel_id=1, source_target_pairs={{64,0},{72,8},{80,16},{88,24},{96,32},{104,40},{112,48},{120,56},{... | collective-permute-start | bytes 1179656 | tf_op jit(solution)/shard_map/ppermute | solution.py:17
  125.9 5.3 %copy-start.19 = (f32[128,4]{0,1:T(4,128)S(1)}, f32[128,4]{0,1:T(4,128)}, u32[]{:S(2)}) copy-start(f32[128,4]{0,1:T(4,128)} %param.15) | copy-start | bytes 6148
  190.8 49.1 %all-to-all-start.3 = ((bf16[16,48,2048]{2,1,0:T(8,128)(2,1)}), bf16[16,48,2048]{2,1,0:T(8,128)(2,1)S(1)}, u32[]{:S(2)}, u32[]{:S(2)}) async-start(bf16[16,48,2048]{2,1,0:T(8,128)(2,1)} %select_select_fusion), calls=%async_computation.3 | async-start | bytes 6291456 | tf_op jit(solution)/shard_map/all_to_all | solution.py:131
  195.2 289.3 %reduce-scatter.2.cloned.1.call-start = ((), (), s32[]{:S(2)}) async-start(), calls=%async_computation.7 | async-start | bytes 10616832 | tf_op jit(solution)/shard_map/reduce_scatter | solution.py:153
  199.1 8.4 %copy-start.4 = (bf16[8,1,2,256,768]{4,3,0,2,1:T(8,128)(2,1)}, bf16[8,1,2,256,768]{4,3,0,2,1:T(8,128)(2,1)S(1)}, u32[]{:S(2)}) copy-start(bf16[8,1,2,256,768]{4,3,0,2,1:T(8,128)(2,1)S(1)} %copy.35) | copy-start | bytes 18874372
  265.9 3.0 copy-start.21
  265.9 3.0 copy-start.20
  265.9 3.0 copy-start.22
  288.8 5.1 %slice-start = ((s8[6291456]{0:T(1024)(128)(4,1)}), s8[2097152]{0:T(1024)(128)(4,1)S(1)}, s32[]{:S(2)}) async-start(s8[6291456]{0:T(1024)(128)(4,1)} %bitcast.112), calls=%async_computation.8 | async-start | bytes 4194304
  288.9 5.1 %slice-start.1 = ((s8[6291456]{0:T(1024)(128)(4,1)}), s8[4194304]{0:T(1024)(128)(4,1)S(1)}, s32[]{:S(2)}) async-start(s8[6291456]{0:T(1024)(128)(4,1)} %bitcast.112), calls=%async_computation.9 | async-start | bytes 8388608
  288.9 5.1 %copy-start.23 = (bf16[768,768]{0,1:T(8,128)(2,1)S(1)}, bf16[768,768]{0,1:T(8,128)(2,1)}, u32[]{:S(2)}) copy-start(bf16[768,768]{0,1:T(8,128)(2,1)} %copy-done.22) | copy-start | bytes 3538948
  298.1 51.2 %all-to-all-start.4 = ((bf16[16,48,2048]{2,1,0:T(8,128)(2,1)}), bf16[16,48,2048]{2,1,0:T(8,128)(2,1)S(1)}, u32[]{:S(2)}, u32[]{:S(2)}) async-start(bf16[16,48,2048]{2,1,0:T(8,128)(2,1)} %bitcast.119), calls=%async_computation.4 | async-start | bytes 6291456 | tf_op jit(solution)/shard_map/all_to_all | solution.py:140
  349.2 46.6 %all-to-all-start.2 = ((bf16[16,48,2048]{2,1,0:T(8,128)(2,1)}), bf16[16,48,2048]{2,1,0:T(8,128)(2,1)}, u32[]{:S(2)}, u32[]{:S(2)}) async-start(bf16[16,48,2048]{2,1,0:T(8,128)(2,1)} %bitcast.116), calls=%async_computation.2 | async-start | bytes 6291456 | tf_op jit(solution)/shard_map/all_to_all | solution.py:114
  354.0 5.4 %copy-start.6 = (f32[1,2,256,768]{3,2,1,0:T(8,128)S(1)}, f32[1,2,256,768]{3,2,1,0:T(8,128)}, u32[]{:S(2)}) copy-start(f32[1,2,256,768]{3,2,1,0:T(8,128)} %param.20) | copy-start | bytes 4718596
  354.0 6.5 %copy-start.12 = (f32[1,768,256]{2,1,0:T(8,128)S(1)}, f32[1,768,256]{2,1,0:T(8,128)}, u32[]{:S(2)}) copy-start(f32[1,768,256]{2,1,0:T(8,128)} %param.21) | copy-start | bytes 2359300
  354.1 10.2 %copy-start.14 = (f32[1,768,256]{2,1,0:T(8,128)S(1)}, f32[1,768,256]{2,1,0:T(8,128)}, u32[]{:S(2)}) copy-start(f32[1,768,256]{2,1,0:T(8,128)} %param.22) | copy-start | bytes 2359300
  356.6 131.1 %collective-permute-start.2 = (bf16[1,2,256,768]{3,2,1,0:T(8,128)(2,1)}, bf16[1,2,256,768]{3,2,1,0:T(8,128)(2,1)}, u32[]{:S(2)}, u32[]{:S(2)}) collective-permute-start(bf16[1,2,256,768]{3,2,1,0:T(8,128)(2,1)} %convert_element_type.94), channel_id=1, source_target_pairs={{64,0},{72,8},{80,16},{88,24},{96,32},{104,40},{112,48},{120,56},{... | collective-permute-start | bytes 2359304 | tf_op jit(solution)/shard_map/ppermute | solution.py:17
  360.4 127.3 %collective-permute-start.3 = (bf16[1,2,256,768]{3,2,1,0:T(8,128)(2,1)}, bf16[1,2,256,768]{3,2,1,0:T(8,128)(2,1)}, u32[]{:S(2)}, u32[]{:S(2)}) collective-permute-start(bf16[1,2,256,768]{3,2,1,0:T(8,128)(2,1)} %convert_element_type.97), channel_id=1, source_target_pairs={{64,0},{72,8},{80,16},{88,24},{96,32},{104,40},{112,48},{120,56},{... | collective-permute-start | bytes 2359304 | tf_op jit(solution)/shard_map/ppermute | solution.py:17
  361.3 133.2 %collective-permute-start.4 = (bf16[1,768,256]{2,1,0:T(8,128)(2,1)}, bf16[1,768,256]{2,1,0:T(8,128)(2,1)}, u32[]{:S(2)}, u32[]{:S(2)}) collective-permute-start(bf16[1,768,256]{2,1,0:T(8,128)(2,1)} %convert_element_type.101), channel_id=1, source_target_pairs={{64,0},{72,8},{80,16},{88,24},{96,32},{104,40},{112,48},{120,56},{... | collective-permute-start | bytes 1179656 | tf_op jit(solution)/shard_map/ppermute | solution.py:17
  365.0 129.6 %collective-permute-start.5 = (bf16[1,768,256]{2,1,0:T(8,128)(2,1)}, bf16[1,768,256]{2,1,0:T(8,128)(2,1)}, u32[]{:S(2)}, u32[]{:S(2)}) collective-permute-start(bf16[1,768,256]{2,1,0:T(8,128)(2,1)} %convert_element_type.103), channel_id=1, source_target_pairs={{64,0},{72,8},{80,16},{88,24},{96,32},{104,40},{112,48},{120,56},{... | collective-permute-start | bytes 1179656 | tf_op jit(solution)/shard_map/ppermute | solution.py:17
  395.9 7.7 %copy-start.2 = (bf16[512,2048]{1,0:T(8,128)(2,1)S(1)}, bf16[512,2048]{1,0:T(8,128)(2,1)}, u32[]{:S(2)}) copy-start(bf16[512,2048]{1,0:T(8,128)(2,1)} %gather_fusion.3) | copy-start | bytes 6291460
  484.5 3.0 copy-start.3
  485.8 1.9 copy-start.10
  487.5 1.4 copy-start.5
  487.5 1.9 copy-start.7
  487.7 6.9 %copy-start.8 = (bf16[1,768,256]{2,1,0:T(8,128)(2,1)S(1)}, bf16[1,768,256]{2,1,0:T(8,128)(2,1)}, u32[]{:S(2)}) copy-start(bf16[1,768,256]{2,1,0:T(8,128)(2,1)} %broadcast_select_fusion.2) | copy-start | bytes 1179652
  487.7 6.9 %copy-start.13 = (f32[1,768,256]{2,1,0:T(8,128)S(1)}, f32[1,768,256]{2,1,0:T(8,128)}, u32[]{:S(2)}) copy-start(f32[1,768,256]{2,1,0:T(8,128)} %param.21) | copy-start | bytes 2359300
  487.7 6.9 %copy-start.15 = (f32[1,768,256]{2,1,0:T(8,128)S(1)}, f32[1,768,256]{2,1,0:T(8,128)}, u32[]{:S(2)}) copy-start(f32[1,768,256]{2,1,0:T(8,128)} %param.22) | copy-start | bytes 2359300
  489.3 8.2 %copy-start.1 = (bf16[128,2048]{1,0:T(8,128)(2,1)S(1)}, bf16[128,2048]{1,0:T(8,128)(2,1)}, u32[]{:S(2)}) copy-start(bf16[128,2048]{1,0:T(8,128)(2,1)} %param.13) | copy-start | bytes 1572868
Sparse Core Ops, SparseCore 0:
  123.0 136.1 all-gather.1
  289.0 195.4 reduce-scatter.1
